TPU v7x, 32 devices: a whole 2x2x4 slice. The times are simulated.
32 devices in a mesh: depth: 4 (over x, core), tile: 8 (over z, y).
Axes of the slice: x: 2, y: 2, z: 4, core: 2. Of those that a mesh axis runs over, the one named last changes fastest.
Arguments:
- density: bfloat16 [64, 256, 1024], P('depth', 'tile'), may hold values from -6 to 6
- row_shift: int32 [64], P('depth'), may hold values from -6 to 6
- brick_order: int32 [4], replicated, may hold values from 0 to 3, as said below
- tf_gain: float32 [4], replicated, may hold values from 0.5 to 2
- tf_bias: float32 [4], replicated, may hold values from -1 to 1
- light_dir: float32 [3], replicated, may hold values from -1 to 1
- background: float32 [3], replicated, may hold values from 0 to 1
Outputs:
- picture: float32 [4, 256, 1024], P(None, 'tile')
Inputs may be any that keep to these rules, and one draw needn't show every extreme that they name: brick_order is a permutation in which, for every bit level l, bit l of brick_order[i] is bit l of i XOR a value that depends only on the bits of i above l.
All inputs are finite; a program needn't handle non-finite values.
Results may differ from a plain program's by a relative error of at most 0.0003.
Values may be sent and summed in bfloat16 or wider, within the bound.
A program may use at most 64 MiB of HBM per device.

v0:
```python
import jax
import jax.numpy as jnp
from jax import lax
from jax.sharding import PartitionSpec as P

MAXS = 6


optical_scale = 1.0


def padded_2(value, sides, width):
    for axis, dim in sides:
        peers, length = (lax.axis_size(axis), value.shape[dim])
        up = [(i, (i + 1) % peers) for i in range(peers - 1)]
        down = [(j, i) for i, j in up]
        last = lax.slice_in_dim(value, length - width, length, axis=dim)
        initial = lax.slice_in_dim(value, 0, width, axis=dim)
        before = lax.ppermute(last, axis, up)
        after = lax.ppermute(initial, axis, down)
        value = jnp.concatenate([before, value, after], axis=dim)
    return value


def from_partner(value, axis, stride):
    mask = 2**stride
    pairs = [(source, source ^ mask) for source in range(lax.axis_size(axis))]
    return lax.ppermute(value, axis, pairs)


def composite_over(front_part, back_part):
    front_colour = front_part[:3]
    front_pass = front_part[3:]
    return jnp.concatenate(
        [front_colour + front_pass * back_part[:3], front_pass * back_part[3:]], 0
    )


def finish_pixels(portion, background):
    shaped = background.reshape((3,) + (1,) * (portion.ndim - 1))
    colour = portion[:3] + portion[3:] * shaped
    return jnp.concatenate([colour, 1.0 - portion[3:]], 0)


def on_device(density, row_shift, brick_order, tf_gain, tf_bias, light_dir, background):
    slice_count, row_count, col_count = density.shape
    depth_count = lax.axis_size("depth")
    swap_rounds = depth_count.bit_length() - 1
    total_slices = slice_count * depth_count
    rim_rows = MAXS + 1
    padded = padded_2(density, (("tile", 1),), rim_rows)
    offsets = rim_rows - 1 - row_shift

    def cut_window(sheet_rows, offset):
        return lax.dynamic_slice_in_dim(sheet_rows, offset, row_count + 2, 0)

    sampled = jax.vmap(cut_window)(padded, offsets).astype(jnp.float32)
    value = sampled[:, 1:-1, :]
    grad_rows = 0.5 * (sampled[:, 2:, :] - sampled[:, :-2, :])
    col_padded = jnp.pad(value, ((0, 0), (0, 0), (1, 1)))
    grad_cols = 0.5 * (col_padded[:, :, 2:] - col_padded[:, :, :-2])
    inverse_norm = lax.rsqrt(1.0 + grad_cols * grad_cols + grad_rows * grad_rows)
    shading = (
        0.25
        + jnp.abs(light_dir[2] - light_dir[0] * grad_cols - light_dir[1] * grad_rows) * inverse_norm
    )
    optical = jax.nn.softplus(tf_gain[3] * value + tf_bias[3]) * (optical_scale / total_slices)
    before = jnp.exp(-(jnp.cumsum(optical, axis=0) - optical))
    weights = before * (1.0 - jnp.exp(-optical))
    channel_sums = [
        jnp.sum(weights * jax.nn.sigmoid(tf_gain[k] * value + tf_bias[k]) * shading, axis=0)
        for k in range(3)
    ]
    through = jnp.exp(-jnp.sum(optical, axis=0))
    partial_image = jnp.stack(channel_sums + [through], 0).reshape(4, row_count * col_count)
    my_index = lax.axis_index("depth")
    my_position = brick_order[my_index]
    portion = partial_image
    for bit_level in range(swap_rounds):
        half_cols = portion.shape[1] // 2
        upper_side = jnp.bitwise_and(jnp.right_shift(my_index, bit_level), 1) == 1
        kept_half = jnp.where(upper_side, portion[:, half_cols:], portion[:, :half_cols])
        sent_half = jnp.where(upper_side, portion[:, :half_cols], portion[:, half_cols:])
        partner = from_partner(sent_half, "depth", bit_level)
        in_front = jnp.bitwise_and(jnp.right_shift(my_position, bit_level), 1) == 0
        portion = jnp.where(
            in_front, composite_over(kept_half, partner), composite_over(partner, kept_half)
        )
    finished = finish_pixels(portion, background)
    gathered = lax.all_gather(finished, "depth", axis=1, tiled=True)
    block_cols = gathered.shape[1] // depth_count
    split_bits = gathered.reshape((4,) + (2,) * swap_rounds + (block_cols,))
    axes_order = (0,) + tuple(range(swap_rounds, 0, -1)) + (swap_rounds + 1,)
    tiles = jnp.transpose(split_bits, axes_order).reshape(4, row_count, col_count)
    return tiles


def solution(mesh):
    placed = (P("depth", "tile", None), P("depth"), P(), P(), P(), P(), P())
    return jax.shard_map(
        on_device, mesh=mesh, in_specs=placed, out_specs=P(None, "tile", None), check_vma=False
    )
```

profile of v0, /device:TPU:9, one launch (start us, length us, event | category | flops | bytes accessed | tf_op | source)
XLA Modules:
  0.0 57.0 jit_solution(14691613299615634390)
XLA Ops:
  0.0 0.0 copy-start
  0.0 0.0 copy-start.1
  0.0 0.0 copy-start.2
  0.0 0.0 copy-start.4
  0.0 1.8 %copy.16 = bf16[16,32,1024]{2,0,1:T(8,128)(2,1)S(1)} copy(bf16[16,32,1024]{2,1,0:T(8,128)(2,1)} %param.7) | data formatting | bytes 2097152 | tf_op args[0]
  1.9 3.1 %collective-permute-start = (bf16[16,7,1024]{2,0,1:T(8,128)(2,1)S(1)}, bf16[16,7,1024]{2,0,1:T(8,128)(2,1)S(1)}, u32[]{:S(2)}, u32[]{:S(2)}) collective-permute-start(bf16[16,7,1024]{2,0,1:T(8,128)(2,1)S(1)} %get-tuple-element.9), channel_id=1, source_target_pairs={{0,1},{1,2},{2,3},{3,4},{4,5},{5,6},{6,7},{8,9},{9,10},{10,11},{11... | collective-permute-start | bytes 688136 | tf_op jit(solution)/shard_map/ppermute | solution.py:19
  5.1 3.0 %collective-permute-start.1 = (bf16[16,7,1024]{2,0,1:T(8,128)(2,1)S(1)}, bf16[16,7,1024]{2,0,1:T(8,128)(2,1)S(1)}, u32[]{:S(2)}, u32[]{:S(2)}) collective-permute-start(bf16[16,7,1024]{2,0,1:T(8,128)(2,1)S(1)} %get-tuple-element.10), channel_id=1, source_target_pairs={{1,0},{2,1},{3,2},{4,3},{5,4},{6,5},{7,6},{9,8},{10,9},{11,10},{12... | collective-permute-start | bytes 688136 | tf_op jit(solution)/shard_map/ppermute | solution.py:20
  8.1 0.0 copy-done
  8.1 0.6 %fusion.15 = (f32[1]{0:T(128)}, f32[1]{0:T(128)}, f32[1]{0:T(128)}, f32[1]{0:T(128)}) fusion(f32[4]{0:T(128)S(1)} %copy-done), kind=kLoop, calls=%fused_computation.47 | loop fusion | bytes 32 | tf_op jit(solution)/shard_map/slice | solution.py:71
  8.7 0.0 copy-done.1
  8.7 0.7 %fusion.16 = (f32[1]{0:T(128)}, f32[1]{0:T(128)}, f32[1]{0:T(128)}, f32[1]{0:T(128)}) fusion(f32[4]{0:T(128)S(1)} %copy-done.1), kind=kLoop, calls=%fused_computation.48 | loop fusion | bytes 32 | tf_op jit(solution)/shard_map/slice | solution.py:71
  9.4 0.0 copy-done.2
  9.4 0.6 %fusion.17 = (f32[1]{0:T(128)}, f32[1]{0:T(128)}, f32[1]{0:T(128)}) fusion(f32[3]{0:T(128)S(1)} %copy-done.2), kind=kLoop, calls=%fused_computation.49 | loop fusion | bytes 24 | tf_op jit(solution)/shard_map/slice | solution.py:65
  11.2 0.0 copy-done.4
  11.2 0.0 collective-permute-done
  11.2 5.9 %collective-permute-done.1 = bf16[16,7,1024]{2,0,1:T(8,128)(2,1)S(1)} collective-permute-done((bf16[16,7,1024]{2,0,1:T(8,128)(2,1)S(1)}, bf16[16,7,1024]{2,0,1:T(8,128)(2,1)S(1)}, u32[]{:S(2)}, u32[]{:S(2)}) %collective-permute-start.1) | collective-permute-done | bytes 229408 | tf_op jit(solution)/shard_map/ppermute | solution.py:20
  17.1 0.2 pad_maximum_fusion
  17.3 3.8 %gather_fusion = bf16[16,34,1024]{2,0,1:T(8,128)(2,1)S(1)} fusion(bf16[16,46,1024]{2,0,1:T(8,128)(2,1)S(1)} %pad_maximum_fusion, s32[16]{0:T(128)S(1)} %fusion.7), kind=kCustom, calls=%fused_computation | custom fusion | bytes 2228416 | tf_op jit(solution)/shard_map/vmap()/gather | solution.py:55
  21.1 0.7 %copy_convert_fusion = f32[16,34,1024]{2,1,0:T(8,128)S(1)} fusion(bf16[16,34,1024]{2,0,1:T(8,128)(2,1)S(1)} %gather_fusion), kind=kLoop, calls=%fused_computation.13 | loop fusion | flops 557056 | bytes 3342336 | tf_op jit(solution)/shard_map/convert_element_type | solution.py:57
  21.8 0.4 slice.148
  22.2 5.0 %subtract_multiply_fusion = f32[16,32,1024]{2,1,0:T(8,128)S(1)} fusion(f32[]{:T(128)} %bitcast.5, f32[]{:T(128)} %bitcast.2, f32[16,34,1024]{2,1,0:T(8,128)S(1)} %copy_convert_fusion), kind=kOutput, calls=%fused_computation.11 | output fusion | flops 19922944 | bytes 6293504 | tf_op jit(solution)/shard_map/jit(cumsum)/reduce_window_sum | solution.py:68
  27.2 10.4 %multiply_reduce_fusion.2 = (f32[32,1024]{1,0:T(8,128)S(1)}, f32[32,1024]{1,0:T(8,128)S(1)}, f32[32,1024]{1,0:T(8,128)S(1)}, f32[32,1024]{1,0:T(8,128)S(1)}) fusion(f32[16,32,1024]{2,1,0:T(8,128)S(1)} %subtract_multiply_fusion, f32[]{:T(128)} %bitcast.7, f32[]{:T(128)} %bitcast.6, f32[16,34,1024]{2,1,0:T(8,128)S(1)} %copy_convert_fusion, f32[]{:T(128)} %bitcast.14, ...), kind=kLoop, calls=%fused_computation.9 | loop fusion | flops 25559040 | bytes 11010092 | tf_op jit(solution)/shard_map/reduce_sum | solution.py:71
  37.6 0.0 copy-start.5
  37.7 0.1 copy.24
  37.8 0.1 copy.21
  38.0 0.1 copy.22
  38.1 0.1 copy.23
  38.3 0.5 pad_maximum_fusion.1
  38.8 0.1 slice_select_fusion.1
  38.9 0.6 collective-permute-start.2
  39.4 0.0 copy-done.5
  39.4 0.6 %dynamic_slice.3 = s32[1]{0:T(128)} dynamic-slice(s32[4]{0:T(128)S(1)} %copy-done.5, s32[]{:T(128)S(6)} %select_n.46), dynamic_slice_sizes={1} | dynamic-slice | bytes 12 | tf_op jit(solution)/shard_map/dynamic_slice | solution.py:77
  40.7 0.0 collective-permute-done.2
  40.7 0.0 copy-start.3
  40.7 0.2 fusion.12
  40.9 0.1 multiply_add_fusion.1
  41.0 0.2 fusion.4
  41.3 1.3 %collective-permute-start.3 = (f32[4,8192]{1,0:T(4,128)S(1)}, f32[4,8192]{1,0:T(4,128)S(1)}, u32[]{:S(2)}, u32[]{:S(2)}) collective-permute-start(f32[4,8192]{1,0:T(4,128)S(1)} %get-tuple-element.18), channel_id=1, source_target_pairs={{0,16},{8,24},{16,0},{24,8},{1,17},{9,25},{17,1},{25,9},{2,18},{10... | collective-permute-start | bytes 393224 | tf_op jit(solution)/shard_map/ppermute | solution.py:28
  43.2 2.9 %collective-permute-done.3 = f32[4,8192]{1,0:T(4,128)S(1)} collective-permute-done((f32[4,8192]{1,0:T(4,128)S(1)}, f32[4,8192]{1,0:T(4,128)S(1)}, u32[]{:S(2)}, u32[]{:S(2)}) %collective-permute-start.3) | collective-permute-done | bytes 131104 | tf_op jit(solution)/shard_map/ppermute | solution.py:28
  46.1 0.1 fusion.14
  46.2 0.1 multiply_add_fusion.3
  46.3 0.1 fusion.5
  46.4 0.1 fusion.13
  46.4 0.0 copy-done.3
  46.5 0.1 slice_add_fusion
  46.6 0.1 pad_maximum_fusion.6
  46.6 8.1 %all_gather.3 = f32[4,32768]{1,0:T(4,128)S(1)} all-gather(f32[4,8192]{1,0:T(4,128)S(1)} %pad_maximum_fusion.6), channel_id=1, replica_groups=mesh['depth'=4,'tile'=8] {'depth'}, dimensions={1}, use_global_device_ids=true | all-gather | bytes 655360 | tf_op jit(solution)/shard_map/all_gather | solution.py:90
  54.8 0.5 reshape.48
  55.3 0.4 copy.20
  55.7 1.2 %reshape.49 = f32[4,32,1024]{2,1,0:T(8,128)} reshape(f32[4,2,2,8192]{3,2,1,0:T(2,128)S(1)} %copy.20) | data formatting | bytes 1048576 | tf_op jit(solution)/shard_map/reshape | solution.py:94
  (4 shorter events, 0.1 us)
Async XLA Ops:
  0.0 8.1 %copy-start = (f32[4]{0:T(128)S(1)}, f32[4]{0:T(128)}, u32[]{:S(2)}) copy-start(f32[4]{0:T(128)} %param.10) | copy-start | bytes 52
  0.0 8.7 %copy-start.1 = (f32[4]{0:T(128)S(1)}, f32[4]{0:T(128)}, u32[]{:S(2)}) copy-start(f32[4]{0:T(128)} %param.11) | copy-start | bytes 52
  0.0 9.4 %copy-start.2 = (f32[3]{0:T(128)S(1)}, f32[3]{0:T(128)}, u32[]{:S(2)}) copy-start(f32[3]{0:T(128)} %param.12) | copy-start | bytes 40
  0.0 11.2 %copy-start.4 = (s32[16]{0:T(128)S(1)}, s32[16]{0:T(128)}, u32[]{:S(2)}) copy-start(s32[16]{0:T(128)} %param.8) | copy-start | bytes 196
  1.9 9.3 %collective-permute-start = (bf16[16,7,1024]{2,0,1:T(8,128)(2,1)S(1)}, bf16[16,7,1024]{2,0,1:T(8,128)(2,1)S(1)}, u32[]{:S(2)}, u32[]{:S(2)}) collective-permute-start(bf16[16,7,1024]{2,0,1:T(8,128)(2,1)S(1)} %get-tuple-element.9), channel_id=1, source_target_pairs={{0,1},{1,2},{2,3},{3,4},{4,5},{5,6},{6,7},{8,9},{9,10},{10,11},{11... | collective-permute-start | bytes 688136 | tf_op jit(solution)/shard_map/ppermute | solution.py:19
  5.1 12.1 %collective-permute-start.1 = (bf16[16,7,1024]{2,0,1:T(8,128)(2,1)S(1)}, bf16[16,7,1024]{2,0,1:T(8,128)(2,1)S(1)}, u32[]{:S(2)}, u32[]{:S(2)}) collective-permute-start(bf16[16,7,1024]{2,0,1:T(8,128)(2,1)S(1)} %get-tuple-element.10), channel_id=1, source_target_pairs={{1,0},{2,1},{3,2},{4,3},{5,4},{6,5},{7,6},{9,8},{10,9},{11,10},{12... | collective-permute-start | bytes 688136 | tf_op jit(solution)/shard_map/ppermute | solution.py:20
  37.6 1.8 %copy-start.5 = (s32[4]{0:T(128)S(1)}, s32[4]{0:T(128)}, u32[]{:S(2)}) copy-start(s32[4]{0:T(128)} %param.9) | copy-start | bytes 52
  38.9 1.8 %collective-permute-start.2 = (f32[4,16384]{1,0:T(4,128)S(1)}, f32[4,16384]{1,0:T(4,128)S(1)}, u32[]{:S(2)}, u32[]{:S(2)}) collective-permute-start(f32[4,16384]{1,0:T(4,128)S(1)} %get-tuple-element.14), channel_id=1, source_target_pairs={{0,8},{8,0},{16,24},{24,16},{1,9},{9,1},{17,25},{25,17},{2,10},{10... | collective-permute-start | bytes 786440 | tf_op jit(solution)/shard_map/ppermute | solution.py:28
  40.7 5.7 %copy-start.3 = (f32[3]{0:T(128)S(1)}, f32[3]{0:T(128)}, u32[]{:S(2)}) copy-start(f32[3]{0:T(128)} %param.13) | copy-start | bytes 40
  41.3 4.9 %collective-permute-start.3 = (f32[4,8192]{1,0:T(4,128)S(1)}, f32[4,8192]{1,0:T(4,128)S(1)}, u32[]{:S(2)}, u32[]{:S(2)}) collective-permute-start(f32[4,8192]{1,0:T(4,128)S(1)} %get-tuple-element.18), channel_id=1, source_target_pairs={{0,16},{8,24},{16,0},{24,8},{1,17},{9,25},{17,1},{25,9},{2,18},{10... | collective-permute-start | bytes 393224 | tf_op jit(solution)/shard_map/ppermute | solution.py:28
where the time goes:
time: 57.3 us; the launch traced here: 57 us
  other arithmetic  17.9 us (31%)
  local copies, waits for them, and re-layouts  11.3 us (20%)
  waiting for transfers between devices  8.82 us (15%)
  blocking collectives  8.13 us (14%)
  starting transfers between devices  8.02 us (14%)
  between operations  2.79 us (5%)
    reduce_sum x1, other arithmetic, on_device(): jnp.sum(weights * jax.nn.sigmoid(tf_gain[k] * value + tf_bias[k]) * shadi...  10.4 us
    all_gather x1, blocking collectives, on_device(): gathered = lax.all_gather(finished, 'depth', axis=1, tiled=True)  8.13 us
    ppermute x1, waiting for transfers between devices, padded_2(): after = lax.ppermute(initial, axis, down)  5.9 us
    another operation x1, other arithmetic, on_device(): before = jnp.exp(-(jnp.cumsum(optical, axis=0) - optical))  4.98 us
    gather x1, local copies, waits for them, and re-layouts, cut_window(): return lax.dynamic_slice_in_dim(sheet_rows, offset, row_count + 2, 0)  3.77 us
    ppermute x1, starting transfers between devices, padded_2(): before = lax.ppermute(last, axis, up)  3.15 us
    ppermute x1, starting transfers between devices, padded_2(): after = lax.ppermute(initial, axis, down)  3.03 us
    ppermute x2, waiting for transfers between devices, from_partner(): return lax.ppermute(value, axis, pairs)  2.92 us
  transfers between devices with their start and end apart: 4, of which 2 were waited for; matrix products, arithmetic and copies ran while one was open for 4% of the time, Pallas kernels for 0%

commit v1 on v0

v1 whole, which is shorter than its diff:
```python
import functools
import math

import jax
import jax.numpy as jnp
from jax import lax
from jax.experimental import pallas as pl
from jax.experimental.pallas import tpu as pltpu
from jax.sharding import PartitionSpec as P

LANES = 128
RIM = 8
MESH = pl.DeviceIdType.MESH


def kernel(
    sizes,
    density,
    row_shift,
    brick_order,
    gain,
    bias,
    light,
    background,
    out,
    ext,
    bundle,
    near,
    far,
    part,
    got,
    comp,
    halo_sems,
    swap_sems,
):
    n_depth, n_tile, halo_chunks = sizes
    slices, rows, cols = density.shape
    levels = n_depth.bit_length() - 1
    blocks = rows // RIM
    half = cols // 2
    half_tiles = half // LANES
    col_tiles = cols // LANES
    total = slices * n_depth
    me_d = lax.axis_index("depth")
    me_t = lax.axis_index("tile")
    odd = lax.rem(me_t, 2)
    pair_t = me_t + 1 - 2 * odd
    low_ok = me_t >= 2
    high_ok = me_t + 2 < n_tile
    is_odd = odd == 1
    sends_on = jnp.logical_or(
        jnp.logical_and(is_odd, low_ok), jnp.logical_and(jnp.logical_not(is_odd), high_ok)
    )
    gets_far = jnp.logical_or(
        jnp.logical_and(is_odd, high_ok), jnp.logical_and(jnp.logical_not(is_odd), low_ok)
    )
    on_t = me_t + 2 - 4 * odd

    def flip(level):
        bit = lax.rem(me_d // (2**level), 2)
        return me_d + (1 - 2 * bit) * 2**level

    barrier = pltpu.get_barrier_semaphore()
    pl.semaphore_signal(barrier, inc=1, device_id={"tile": pair_t}, device_id_type=MESH)
    for level in range(levels):
        pl.semaphore_signal(barrier, inc=1, device_id={"depth": flip(level)}, device_id_type=MESH)

    @pl.when(low_ok)
    def _():
        pl.semaphore_signal(barrier, inc=1, device_id={"tile": me_t - 2}, device_id_type=MESH)

    @pl.when(high_ok)
    def _():
        pl.semaphore_signal(barrier, inc=1, device_id={"tile": me_t + 2}, device_id_type=MESH)

    place = lax.broadcasted_iota(jnp.int32, (RIM, cols), 0)

    def build(g, _):
        picked = []
        for i in range(2):
            j = 2 * g + i
            shift = row_shift[j]
            first = density[j, 0:16, :].astype(jnp.float32)[0:RIM]
            last = density[j, rows - 16 : rows, :].astype(jnp.float32)[16 - RIM :]
            use_last = jnp.where(shift > 0, 0, jnp.where(shift < 0, RIM, RIM // 2))
            picked.append(jnp.where(place >= use_last, last, first))
        bundle[g] = jnp.concatenate(picked, 0).astype(bundle.dtype)
        return 0

    lax.fori_loop(0, slices // 2, build, 0)

    peers = 1 + levels + low_ok.astype(jnp.int32) + high_ok.astype(jnp.int32)
    pl.semaphore_wait(barrier, peers)

    per = slices // 2 // halo_chunks
    near_copies = []
    far_copies = []
    for c in range(halo_chunks):
        span = pl.ds(c * per, per)
        near_copies.append(
            pltpu.make_async_remote_copy(
                src_ref=bundle.at[span],
                dst_ref=near.at[span],
                send_sem=halo_sems.at[0, c],
                recv_sem=halo_sems.at[1, c],
                device_id={"tile": pair_t},
                device_id_type=MESH,
            )
        )
        far_copies.append(
            pltpu.make_async_remote_copy(
                src_ref=near.at[span],
                dst_ref=far.at[span],
                send_sem=halo_sems.at[2, c],
                recv_sem=halo_sems.at[3, c],
                device_id={"tile": on_t},
                device_id_type=MESH,
            )
        )
        near_copies[-1].start()

    @pl.when(jnp.logical_not(gets_far))
    def _():
        far[...] = jnp.zeros_like(far)

    def fill(j, _):
        sheet = density[j].astype(jnp.float32)
        for t in range(col_tiles):
            ext[j, t, RIM : RIM + rows, :] = sheet[:, t * LANES : (t + 1) * LANES]
        return 0

    lax.fori_loop(0, slices, fill, 0)

    def pass_on(c):
        near_copies[c].wait_recv()

        @pl.when(sends_on)
        def _():
            far_copies[c].start()

    lane = lax.broadcasted_iota(jnp.int32, (RIM, LANES), 1)
    is_first = lane == 0
    is_last = lane == LANES - 1
    log2e = math.log2(math.e)
    half_gain = [0.5 * gain[k] for k in range(3)]
    half_bias = [0.5 * bias[k] for k in range(3)]
    opt_gain = gain[3] * log2e
    opt_bias = bias[3] * log2e
    light_c = 0.5 * light[0]
    light_r = 0.5 * light[1]
    light_z = light[2]

    def render(block, side):
        def step(j, carry):
            base = RIM + block * RIM - 1 - row_shift[j]
            tiles = range(side * half_tiles - 1, (side + 1) * half_tiles + 1)
            value = [
                ext[j, t, pl.ds(base + 1, RIM), :] if 0 <= t < col_tiles else None for t in tiles
            ]
            zero = jnp.zeros((RIM, LANES), jnp.float32)
            value = [zero if v is None else v for v in value]
            new = []
            for i in range(half_tiles):
                t = side * half_tiles + i
                through, base_sum, c0, c1, c2 = carry[i]
                v = value[i + 1]
                above = ext[j, t, pl.ds(base, RIM), :]
                below = ext[j, t, pl.ds(base + 2, RIM), :]
                left = pltpu.roll(jnp.where(is_last, value[i], v), 1, 1)
                right = pltpu.roll(jnp.where(is_first, value[i + 2], v), LANES - 1, 1)
                drow = below - above
                dcol = right - left
                norm = lax.rsqrt(4.0 + (dcol * dcol + drow * drow))
                shade = 0.125 + jnp.abs(light_z - light_c * dcol - light_r * drow) * norm
                grow = jnp.exp2(opt_gain * v + opt_bias)
                passed = jnp.exp2(jnp.log(1.0 + grow) * (-log2e / total))
                after = through * passed
                weight = (through - after) * shade
                sums = [
                    c + weight * jnp.tanh(half_gain[k] * v + half_bias[k])
                    for k, c in enumerate((c0, c1, c2))
                ]
                new.append((after, base_sum + weight, *sums))
            return tuple(new)

        zero = jnp.zeros((RIM, LANES), jnp.float32)
        one = jnp.ones((RIM, LANES), jnp.float32)
        start = tuple((one, zero, zero, zero, zero) for _ in range(half_tiles))
        done = lax.fori_loop(0, slices, step, start)
        for i in range(half_tiles):
            through, base_sum, *sums = done[i]
            at = slice(i * LANES, (i + 1) * LANES)
            for k in range(3):
                part[block, side, k, :, at] = base_sum + sums[k]
            part[block, side, 3, :, at] = through

    side_bit = lax.rem(me_d, 2)
    position = brick_order[me_d]

    def swap(level, block):
        if level == 0:
            source = part.at[block, 1 - side_bit]
        else:
            source = comp.at[level - 1, block]
        return pltpu.make_async_remote_copy(
            src_ref=source,
            dst_ref=got.at[level, block],
            send_sem=swap_sems.at[0, level, block],
            recv_sem=swap_sems.at[1, level, block],
            device_id={"depth": flip(level if level < levels else 0)},
            device_id_type=MESH,
        )

    def merge(level, block):
        swap(level, block).wait_recv()
        mine = part[block, side_bit] if level == 0 else comp[level - 1, block]
        theirs = got[level, block]
        front = lax.rem(position // (2**level), 2) == 0
        near_part = jnp.where(front, mine, theirs)
        far_part = jnp.where(front, theirs, mine)
        through = near_part[3]
        colour = [near_part[k] + through * far_part[k] for k in range(3)]
        through = through * far_part[3]
        if level == levels - 1:
            colour = [colour[k] + through * background[k] for k in range(3)]
            through = 1.0 - through
        for k in range(3):
            comp[level, block, k] = colour[k]
        comp[level, block, 3] = through
        swap(level + 1, block).start()

    inner = list(range(1, blocks - 1))
    order = inner + [0, blocks - 1]
    pending = []
    passed_on = 0
    for n, block in enumerate(inner):
        for side in range(2):
            render(block, side)
            if passed_on < halo_chunks:
                pass_on(passed_on)
                passed_on += 1
        swap(0, block).start()
        pending.append(block)
        if len(pending) > 1:
            merge(0, pending.pop(0))
    for c in range(passed_on, halo_chunks):
        pass_on(c)

    for c in range(halo_chunks):

        @pl.when(gets_far)
        def _():
            far_copies[c].wait_recv()

        def fill_rim(g, _):
            near_rows = near[g].astype(jnp.float32)
            far_rows = far[g].astype(jnp.float32)
            above = jnp.where(is_odd, near_rows, far_rows)
            below = jnp.where(is_odd, far_rows, near_rows)
            for i in range(2):
                for t in range(col_tiles):
                    at = slice(t * LANES, (t + 1) * LANES)
                    rim = slice(i * RIM, (i + 1) * RIM)
                    ext[2 * g + i, t, 0:RIM, :] = above[rim, at]
                    ext[2 * g + i, t, RIM + rows : 2 * RIM + rows, :] = below[rim, at]
            return 0

        lax.fori_loop(c * per, (c + 1) * per, fill_rim, 0)

    for block in order[len(inner) :]:
        for side in range(2):
            render(block, side)
        swap(0, block).start()
        pending.append(block)
        merge(0, pending.pop(0))
    for block in pending:
        merge(0, block)
    for level in range(1, levels):
        for block in order:
            merge(level, block)
    for block in order:
        swap(levels, block).wait_recv()
        at = pl.ds(block * RIM, RIM)
        mine = comp[levels - 1, block]
        theirs = got[levels, block]
        upper = side_bit == 1
        out[:, at, 0:half] = jnp.where(upper, theirs, mine)
        out[:, at, half:cols] = jnp.where(upper, mine, theirs)

    for c in range(halo_chunks):
        near_copies[c].wait_send()

        @pl.when(sends_on)
        def _():
            far_copies[c].wait_send()

    for level in range(levels + 1):
        for block in order:
            swap(level, block).wait_send()


def on_device(
    density, row_shift, brick_order, tf_gain, tf_bias, light_dir, background, *, n_depth, n_tile
):
    slices, rows, cols = density.shape
    levels = n_depth.bit_length() - 1
    blocks = rows // RIM
    halo_chunks = 4
    smem = pl.BlockSpec(memory_space=pltpu.SMEM)
    vmem = pl.BlockSpec(memory_space=pltpu.VMEM)
    halo = pltpu.VMEM((slices // 2, 2 * RIM, cols), density.dtype)
    image = (4, RIM, cols // 2)
    return pl.pallas_call(
        functools.partial(kernel, (n_depth, n_tile, halo_chunks)),
        out_shape=jax.ShapeDtypeStruct((4, rows, cols), jnp.float32),
        in_specs=[vmem] + [smem] * 6,
        out_specs=vmem,
        scratch_shapes=[
            pltpu.VMEM((slices, cols // LANES, rows + 2 * RIM, LANES), jnp.float32),
            halo,
            halo,
            halo,
            pltpu.VMEM((blocks, 2) + image, jnp.float32),
            pltpu.VMEM((levels + 1, blocks) + image, jnp.float32),
            pltpu.VMEM((levels, blocks) + image, jnp.float32),
            pltpu.SemaphoreType.DMA((4, halo_chunks)),
            pltpu.SemaphoreType.DMA((2, levels + 1, blocks)),
        ],
        compiler_params=pltpu.CompilerParams(collective_id=0, has_side_effects=True),
    )(density, row_shift, brick_order, tf_gain, tf_bias, light_dir, background)


def solution(mesh):
    placed = (P("depth", "tile", None), P("depth"), P(), P(), P(), P(), P())
    body = functools.partial(
        on_device, n_depth=mesh.shape["depth"], n_tile=mesh.shape["tile"]
    )
    return jax.shard_map(
        body, mesh=mesh, in_specs=placed, out_specs=P(None, "tile", None), check_vma=False
    )
```

time: 57.3 us -> 30.4 us (0.53)
  the two profiles are of different devices: /device:TPU:9 before, /device:TPU:13 now
where the time goes in v1:
time: 30.4 us; the launch traced here: 30.2 us
  Pallas kernels  28.3 us (93%)
  local copies, waits for them, and re-layouts  1.89 us (6%)
    pallas_call x1, Pallas kernels, on_device(): pl.pallas_call(functools.partial(kernel, (n_depth, n_tile, halo_chunks)),...  28.3 us
    unnamed x1, local copies, waits for them, and re-layouts  1.89 us

profile of v1, /device:TPU:13, one launch (start us, length us, event | category | flops | bytes accessed | tf_op | source)
XLA Modules:
  0.0 30.2 jit_solution(4821882837413664416)
XLA Ops:
  0.0 28.3 %shard_map.73 = f32[4,32,1024]{2,1,0:T(8,128)} custom-call(bf16[16,32,1024]{2,1,0:T(8,128)(2,1)} %density.1, s32[16]{0:T(128)} %row_shift.1, s32[4]{0:T(128)} %brick_order.1, f32[4]{0:T(128)} %gain.1, f32[4]{0:T(128)} %bias.1, f32[3]{0:T(128)} %light.1, f32[3]{0:T(128)} %background.1), custom_call_target="tpu_custom_call" | custom-call | tf_op jit(solution)/shard_map/pallas_call | solution.py:313
  28.4 1.9 %copy.9 = f32[4,32,1024]{2,1,0:T(8,128)} copy(f32[4,32,1024]{2,1,0:T(8,128)} %shard_map.73) | data formatting | bytes 1048576

commit v2 on v1

--- a/solution.py
+++ b/solution.py
@@ -15,14 +15,22 @@
 
 def kernel(
     sizes,
-    density,
+    stored,
+    row_shift_arg,
+    brick_order_arg,
+    gain_arg,
+    bias_arg,
+    light_arg,
+    background_arg,
+    out,
     row_shift,
     brick_order,
     gain,
     bias,
     light,
     background,
-    out,
+    density,
+    state,
     ext,
     bundle,
     near,
@@ -30,6 +38,8 @@
     part,
     got,
     comp,
+    load_sems,
+    small_sems,
     halo_sems,
     swap_sems,
 ):
@@ -60,6 +70,30 @@
         bit = lax.rem(me_d // (2**level), 2)
         return me_d + (1 - 2 * bit) * 2**level
 
+    loads = [
+        pltpu.make_async_copy(
+            stored.at[:, pl.ds(at, size)], density.at[:, pl.ds(at, size)], load_sems.at[i]
+        )
+        for i, (at, size) in enumerate(
+            [(0, RIM), (rows - RIM, RIM), (RIM, rows - 2 * RIM)]
+        )
+    ]
+    small = [
+        pltpu.make_async_copy(arg, held, small_sems.at[i])
+        for i, (arg, held) in enumerate(
+            [
+                (row_shift_arg, row_shift),
+                (brick_order_arg, brick_order),
+                (gain_arg, gain),
+                (bias_arg, bias),
+                (light_arg, light),
+                (background_arg, background),
+            ]
+        )
+    ]
+    for load in small + loads:
+        load.start()
+
     barrier = pltpu.get_barrier_semaphore()
     pl.semaphore_signal(barrier, inc=1, device_id={"tile": pair_t}, device_id_type=MESH)
     for level in range(levels):
@@ -80,13 +114,15 @@
         for i in range(2):
             j = 2 * g + i
             shift = row_shift[j]
-            first = density[j, 0:16, :].astype(jnp.float32)[0:RIM]
-            last = density[j, rows - 16 : rows, :].astype(jnp.float32)[16 - RIM :]
+            first = density[j, 0:RIM, :].astype(jnp.float32)
+            last = density[j, rows - RIM : rows, :].astype(jnp.float32)
             use_last = jnp.where(shift > 0, 0, jnp.where(shift < 0, RIM, RIM // 2))
             picked.append(jnp.where(place >= use_last, last, first))
         bundle[g] = jnp.concatenate(picked, 0).astype(bundle.dtype)
         return 0
 
+    for load in small + loads[:2]:
+        load.wait()
     lax.fori_loop(0, slices // 2, build, 0)
 
     peers = 1 + levels + low_ok.astype(jnp.int32) + high_ok.astype(jnp.int32)
@@ -123,10 +159,14 @@
     def _():
         far[...] = jnp.zeros_like(far)
 
+    loads[2].wait()
+
     def fill(j, _):
         sheet = density[j].astype(jnp.float32)
+        ext[j, 0] = jnp.zeros((rows + 2 * RIM, LANES), jnp.float32)
+        ext[j, col_tiles + 1] = jnp.zeros((rows + 2 * RIM, LANES), jnp.float32)
         for t in range(col_tiles):
-            ext[j, t, RIM : RIM + rows, :] = sheet[:, t * LANES : (t + 1) * LANES]
+            ext[j, t + 1, RIM : RIM + rows, :] = sheet[:, t * LANES : (t + 1) * LANES]
         return 0
 
     lax.fori_loop(0, slices, fill, 0)
@@ -150,18 +190,14 @@
     light_r = 0.5 * light[1]
     light_z = light[2]
 
-    def render(block, side):
+    def advance(block, side, low, high, carry):
         def step(j, carry):
             base = RIM + block * RIM - 1 - row_shift[j]
-            tiles = range(side * half_tiles - 1, (side + 1) * half_tiles + 1)
-            value = [
-                ext[j, t, pl.ds(base + 1, RIM), :] if 0 <= t < col_tiles else None for t in tiles
-            ]
-            zero = jnp.zeros((RIM, LANES), jnp.float32)
-            value = [zero if v is None else v for v in value]
+            first_tile = side * half_tiles
+            value = [ext[j, first_tile + i, pl.ds(base + 1, RIM), :] for i in range(half_tiles + 2)]
             new = []
             for i in range(half_tiles):
-                t = side * half_tiles + i
+                t = first_tile + i + 1
                 through, base_sum, c0, c1, c2 = carry[i]
                 v = value[i + 1]
                 above = ext[j, t, pl.ds(base, RIM), :]
@@ -183,16 +219,48 @@
                 new.append((after, base_sum + weight, *sums))
             return tuple(new)
 
-        zero = jnp.zeros((RIM, LANES), jnp.float32)
-        one = jnp.ones((RIM, LANES), jnp.float32)
-        start = tuple((one, zero, zero, zero, zero) for _ in range(half_tiles))
-        done = lax.fori_loop(0, slices, step, start)
+        return lax.fori_loop(low, high, step, carry, unroll=4)
+
+    def finish(block, side, carry):
         for i in range(half_tiles):
-            through, base_sum, *sums = done[i]
+            through, base_sum, *sums = carry[i]
             at = slice(i * LANES, (i + 1) * LANES)
             for k in range(3):
                 part[block, side, k, :, at] = base_sum + sums[k]
             part[block, side, 3, :, at] = through
+
+    zero = jnp.zeros((RIM, LANES), jnp.float32)
+    one = jnp.ones((RIM, LANES), jnp.float32)
+    start = tuple((one, zero, zero, zero, zero) for _ in range(half_tiles))
+
+    def render(block):
+        def one_side(side, _):
+            finish(block, side, advance(block, side, 0, slices, start))
+            return 0
+
+        lax.fori_loop(0, 2, one_side, 0)
+
+    def render_rim(c):
+        def one_piece(piece, _):
+            rim = piece // 2
+            side = lax.rem(piece, 2)
+            block = rim * (blocks - 1)
+            if c == 0:
+                carry = start
+            else:
+                carry = tuple(
+                    tuple(state[piece, i, k] for k in range(5)) for i in range(half_tiles)
+                )
+            carry = advance(block, side, c * per * 2, (c + 1) * per * 2, carry)
+            if c == halo_chunks - 1:
+                finish(block, side, carry)
+            else:
+                for i in range(half_tiles):
+                    for k in range(5):
+                        state[piece, i, k] = carry[i][k]
+            return 0
+
+        lax.fori_loop(0, 4, one_piece, 0)
 
     side_bit = lax.rem(me_d, 2)
     position = brick_order[me_d]
@@ -222,8 +290,8 @@
         colour = [near_part[k] + through * far_part[k] for k in range(3)]
         through = through * far_part[3]
         if level == levels - 1:
-            colour = [colour[k] + through * background[k] for k in range(3)]
-            through = 1.0 - through
+            colour = [0.5 * (colour[k] + through * background[k]) for k in range(3)]
+            through = 0.5 - 0.5 * through
         for k in range(3):
             comp[level, block, k] = colour[k]
         comp[level, block, 3] = through
@@ -231,22 +299,21 @@
 
     inner = list(range(1, blocks - 1))
     order = inner + [0, blocks - 1]
-    pending = []
     passed_on = 0
     for n, block in enumerate(inner):
-        for side in range(2):
-            render(block, side)
-            if passed_on < halo_chunks:
-                pass_on(passed_on)
-                passed_on += 1
+        render(block)
         swap(0, block).start()
-        pending.append(block)
-        if len(pending) > 1:
-            merge(0, pending.pop(0))
-    for c in range(passed_on, halo_chunks):
-        pass_on(c)
+        if n > 0:
+            merge(0, inner[n - 1])
+        if passed_on < halo_chunks - 1:
+            pass_on(passed_on)
+            passed_on += 1
+    merge(0, inner[-1])
 
     for c in range(halo_chunks):
+        if c + 1 >= passed_on and passed_on < halo_chunks:
+            pass_on(passed_on)
+            passed_on += 1
 
         @pl.when(gets_far)
         def _():
@@ -261,22 +328,21 @@
                 for t in range(col_tiles):
                     at = slice(t * LANES, (t + 1) * LANES)
                     rim = slice(i * RIM, (i + 1) * RIM)
-                    ext[2 * g + i, t, 0:RIM, :] = above[rim, at]
-                    ext[2 * g + i, t, RIM + rows : 2 * RIM + rows, :] = below[rim, at]
+                    ext[2 * g + i, t + 1, 0:RIM, :] = above[rim, at]
+                    ext[2 * g + i, t + 1, RIM + rows : 2 * RIM + rows, :] = below[rim, at]
             return 0
 
         lax.fori_loop(c * per, (c + 1) * per, fill_rim, 0)
-
-    for block in order[len(inner) :]:
-        for side in range(2):
-            render(block, side)
+        render_rim(c)
+
+    outer = [0, blocks - 1]
+    for block in outer:
         swap(0, block).start()
-        pending.append(block)
-        merge(0, pending.pop(0))
-    for block in pending:
-        merge(0, block)
     for level in range(1, levels):
-        for block in order:
+        for block in inner:
+            merge(level, block)
+    for level in range(levels):
+        for block in outer:
             merge(level, block)
     for block in order:
         swap(levels, block).wait_recv()
@@ -306,28 +372,36 @@
     levels = n_depth.bit_length() - 1
     blocks = rows // RIM
     halo_chunks = 4
-    smem = pl.BlockSpec(memory_space=pltpu.SMEM)
     vmem = pl.BlockSpec(memory_space=pltpu.VMEM)
     halo = pltpu.VMEM((slices // 2, 2 * RIM, cols), density.dtype)
     image = (4, RIM, cols // 2)
-    return pl.pallas_call(
+    small_args = (row_shift, brick_order, tf_gain, tf_bias, light_dir, background)
+    scaled = pl.pallas_call(
         functools.partial(kernel, (n_depth, n_tile, halo_chunks)),
         out_shape=jax.ShapeDtypeStruct((4, rows, cols), jnp.float32),
-        in_specs=[vmem] + [smem] * 6,
+        in_specs=[pl.BlockSpec(memory_space=pltpu.HBM)] * 7,
         out_specs=vmem,
         scratch_shapes=[
-            pltpu.VMEM((slices, cols // LANES, rows + 2 * RIM, LANES), jnp.float32),
+            *[pltpu.SMEM(arg.shape, arg.dtype) for arg in small_args],
+            pltpu.VMEM(density.shape, density.dtype),
+            pltpu.VMEM((4, cols // 2 // LANES, 5, RIM, LANES), jnp.float32),
+            pltpu.VMEM((slices, cols // LANES + 2, rows + 2 * RIM, LANES), jnp.float32),
             halo,
             halo,
             halo,
             pltpu.VMEM((blocks, 2) + image, jnp.float32),
             pltpu.VMEM((levels + 1, blocks) + image, jnp.float32),
             pltpu.VMEM((levels, blocks) + image, jnp.float32),
+            pltpu.SemaphoreType.DMA((3,)),
+            pltpu.SemaphoreType.DMA((len(small_args),)),
             pltpu.SemaphoreType.DMA((4, halo_chunks)),
             pltpu.SemaphoreType.DMA((2, levels + 1, blocks)),
         ],
-        compiler_params=pltpu.CompilerParams(collective_id=0, has_side_effects=True),
-    )(density, row_shift, brick_order, tf_gain, tf_bias, light_dir, background)
+        compiler_params=pltpu.CompilerParams(
+            collective_id=0, has_side_effects=True, vmem_limit_bytes=20 * 2**20
+        ),
+    )(*[pltpu.with_memory_space_constraint(arg, pltpu.HBM) for arg in (density, *small_args)])
+    return scaled + scaled
 
 
 def solution(mesh):

time: 30.4 us -> 23.5 us (0.77)
  Pallas kernels: 28.3 us -> 22.4 us
  local copies, waits for them, and re-layouts: 1.89 us -> 0 us
  other arithmetic: 0 us -> 0.86 us
    pallas_call x1, Pallas kernels: 28.3 us -> 22.4 us  [on_device(): pl.pallas_call(functools.partial(kernel, (n_depth, n_tile, halo_chunks)),...]
    unnamed x1 -> x0, local copies, waits for them, and re-layouts: 1.89 us -> none
    add x0 -> x1, other arithmetic: none -> 0.86 us  [on_device(): return scaled + scaled]
where the time goes in v2:
time: 23.5 us; the launch traced here: 23.3 us
  Pallas kernels  22.4 us (95%)
  other arithmetic  0.86 us (4%)
    pallas_call x1, Pallas kernels, on_device(): pl.pallas_call(functools.partial(kernel, (n_depth, n_tile, halo_chunks)),...  22.4 us
    add x1, other arithmetic, on_device(): return scaled + scaled  0.86 us

profile of v2, /device:TPU:13, one launch (start us, length us, event | category | flops | bytes accessed | tf_op | source)
XLA Modules:
  0.0 23.3 jit_solution(8289610883015433216)
XLA Ops:
  0.0 22.4 %shard_map.73 = f32[4,32,1024]{2,1,0:T(8,128)S(1)} custom-call(bf16[16,32,1024]{2,1,0:T(8,128)(2,1)} %stored.1, s32[16]{0:T(128)} %row_shift_arg.1, s32[4]{0:T(128)} %brick_order_arg.1, f32[4]{0:T(128)} %gain_arg.1, f32[4]{0:T(128)} %bias_arg.1, f32[3]{0:T(128)} %light_arg.1, f32[3]{0:T(128)} %background_arg.1), custom_call_target="tpu_custom_call" | custom-call | tf_op jit(solution)/shard_map/pallas_call | solution.py:379
  22.4 0.9 %add.3 = f32[4,32,1024]{2,1,0:T(8,128)} add(f32[4,32,1024]{2,1,0:T(8,128)S(1)} %shard_map.73, f32[4,32,1024]{2,1,0:T(8,128)S(1)} %shard_map.73) | non-fusion elementwise | flops 131072 | bytes 1572864 | tf_op jit(solution)/shard_map/add | solution.py:404

commit v3 on v2

--- a/solution.py
+++ b/solution.py
@@ -219,7 +219,7 @@
                 new.append((after, base_sum + weight, *sums))
             return tuple(new)
 
-        return lax.fori_loop(low, high, step, carry, unroll=4)
+        return lax.fori_loop(low, high, step, carry, unroll=min(4, high - low))
 
     def finish(block, side, carry):
         for i in range(half_tiles):
@@ -241,10 +241,8 @@
         lax.fori_loop(0, 2, one_side, 0)
 
     def render_rim(c):
-        def one_piece(piece, _):
-            rim = piece // 2
+        def one_piece(piece, block):
             side = lax.rem(piece, 2)
-            block = rim * (blocks - 1)
             if c == 0:
                 carry = start
             else:
@@ -258,9 +256,12 @@
                 for i in range(half_tiles):
                     for k in range(5):
                         state[piece, i, k] = carry[i][k]
-            return 0
-
-        lax.fori_loop(0, 4, one_piece, 0)
+            return block
+
+        for rim, block in enumerate(outer):
+            lax.fori_loop(2 * rim, 2 * rim + 2, one_piece, block)
+            if c == halo_chunks - 1:
+                swap(0, block).start()
 
     side_bit = lax.rem(me_d, 2)
     position = brick_order[me_d]
@@ -290,15 +291,16 @@
         colour = [near_part[k] + through * far_part[k] for k in range(3)]
         through = through * far_part[3]
         if level == levels - 1:
-            colour = [0.5 * (colour[k] + through * background[k]) for k in range(3)]
-            through = 0.5 - 0.5 * through
+            colour = [colour[k] + through * background[k] for k in range(3)]
+            through = 1.0 - through
         for k in range(3):
             comp[level, block, k] = colour[k]
         comp[level, block, 3] = through
         swap(level + 1, block).start()
 
     inner = list(range(1, blocks - 1))
-    order = inner + [0, blocks - 1]
+    outer = [0, blocks - 1]
+    order = inner + outer
     passed_on = 0
     for n, block in enumerate(inner):
         render(block)
@@ -310,10 +312,10 @@
             passed_on += 1
     merge(0, inner[-1])
 
+    for c in range(passed_on, halo_chunks):
+        pass_on(c)
+
     for c in range(halo_chunks):
-        if c + 1 >= passed_on and passed_on < halo_chunks:
-            pass_on(passed_on)
-            passed_on += 1
 
         @pl.when(gets_far)
         def _():
@@ -335,9 +337,6 @@
         lax.fori_loop(c * per, (c + 1) * per, fill_rim, 0)
         render_rim(c)
 
-    outer = [0, blocks - 1]
-    for block in outer:
-        swap(0, block).start()
     for level in range(1, levels):
         for block in inner:
             merge(level, block)
@@ -365,6 +364,12 @@
             swap(level, block).wait_send()
 
 
+def store(held, out, sem):
+    copy = pltpu.make_async_copy(held, out, sem)
+    copy.start()
+    copy.wait()
+
+
 def on_device(
     density, row_shift, brick_order, tf_gain, tf_bias, light_dir, background, *, n_depth, n_tile
 ):
@@ -376,7 +381,7 @@
     halo = pltpu.VMEM((slices // 2, 2 * RIM, cols), density.dtype)
     image = (4, RIM, cols // 2)
     small_args = (row_shift, brick_order, tf_gain, tf_bias, light_dir, background)
-    scaled = pl.pallas_call(
+    picture = pl.pallas_call(
         functools.partial(kernel, (n_depth, n_tile, halo_chunks)),
         out_shape=jax.ShapeDtypeStruct((4, rows, cols), jnp.float32),
         in_specs=[pl.BlockSpec(memory_space=pltpu.HBM)] * 7,
@@ -401,7 +406,14 @@
             collective_id=0, has_side_effects=True, vmem_limit_bytes=20 * 2**20
         ),
     )(*[pltpu.with_memory_space_constraint(arg, pltpu.HBM) for arg in (density, *small_args)])
-    return scaled + scaled
+    return pl.pallas_call(
+        store,
+        out_shape=jax.ShapeDtypeStruct((4, rows, cols), jnp.float32),
+        in_specs=[vmem],
+        out_specs=pl.BlockSpec(memory_space=pltpu.HBM),
+        scratch_shapes=[pltpu.SemaphoreType.DMA],
+        compiler_params=pltpu.CompilerParams(vmem_limit_bytes=2**20),
+    )(picture)
 
 
 def solution(mesh):

time: 23.5 us -> 22.2 us (0.945)
  other arithmetic: 0.86 us -> 0 us
  Pallas kernels: 22.4 us -> 22.1 us
    pallas_call x1, Pallas kernels: 22.4 us -> 21.3 us  [on_device(): pl.pallas_call(functools.partial(kernel, (n_depth, n_tile, halo_chunks)),...]
    add x1 -> x0, other arithmetic: 0.86 us -> none  [on_device(): return scaled + scaled]
    pallas_call x0 -> x1, Pallas kernels: none -> 0.8 us  [on_device(): pl.pallas_call(store, out_shape=jax.ShapeDtypeStruct((4, rows, cols), jnp...]
where the time goes in v3:
time: 22.2 us; the launch traced here: 22.1 us
  Pallas kernels  22.1 us (100%)
    pallas_call x1, Pallas kernels, on_device(): pl.pallas_call(functools.partial(kernel, (n_depth, n_tile, halo_chunks)),...  21.3 us
    pallas_call x1, Pallas kernels, on_device(): pl.pallas_call(store, out_shape=jax.ShapeDtypeStruct((4, rows, cols), jnp...  0.8 us

profile of v3, /device:TPU:13, one launch (start us, length us, event | category | flops | bytes accessed | tf_op | source)
XLA Modules:
  0.0 22.1 jit_solution(11962687054828634999)
XLA Ops:
  0.0 21.3 %shard_map.73.held = f32[4,32,1024]{2,1,0:T(8,128)S(1)} custom-call(bf16[16,32,1024]{2,1,0:T(8,128)(2,1)} %stored.1, s32[16]{0:T(128)} %row_shift_arg.1, s32[4]{0:T(128)} %brick_order_arg.1, f32[4]{0:T(128)} %gain_arg.1, f32[4]{0:T(128)} %bias_arg.1, f32[3]{0:T(128)} %light_arg.1, f32[3]{0:T(128)} %background_arg.1), custom_call_target="tpu_custom_call" | custom-call | tf_op jit(solution)/shard_map/pallas_call | solution.py:384
  21.3 0.8 %shard_map.74 = f32[4,32,1024]{2,1,0:T(8,128)} custom-call(f32[4,32,1024]{2,1,0:T(8,128)S(1)} %shard_map.73.held), custom_call_target="tpu_custom_call" | custom-call | tf_op jit(solution)/shard_map/pallas_call | solution.py:409

commit v4 on v3

--- a/solution.py
+++ b/solution.py
@@ -128,11 +128,14 @@
     peers = 1 + levels + low_ok.astype(jnp.int32) + high_ok.astype(jnp.int32)
     pl.semaphore_wait(barrier, peers)
 
-    per = slices // 2 // halo_chunks
+    quarter = slices // 2 // 4
+    shift_size = quarter // 2
+    starts = [0, quarter + shift_size, 2 * quarter + shift_size, 3 * quarter + shift_size]
+    starts.append(slices // 2)
     near_copies = []
     far_copies = []
     for c in range(halo_chunks):
-        span = pl.ds(c * per, per)
+        span = pl.ds(starts[c], starts[c + 1] - starts[c])
         near_copies.append(
             pltpu.make_async_remote_copy(
                 src_ref=bundle.at[span],
@@ -219,7 +222,7 @@
                 new.append((after, base_sum + weight, *sums))
             return tuple(new)
 
-        return lax.fori_loop(low, high, step, carry, unroll=min(4, high - low))
+        return lax.fori_loop(low, high, step, carry, unroll=next(u for u in (4, 3, 2, 1) if (high - low) % u == 0))
 
     def finish(block, side, carry):
         for i in range(half_tiles):
@@ -249,7 +252,7 @@
                 carry = tuple(
                     tuple(state[piece, i, k] for k in range(5)) for i in range(half_tiles)
                 )
-            carry = advance(block, side, c * per * 2, (c + 1) * per * 2, carry)
+            carry = advance(block, side, 2 * starts[c], 2 * starts[c + 1], carry)
             if c == halo_chunks - 1:
                 finish(block, side, carry)
             else:
@@ -334,7 +337,7 @@
                     ext[2 * g + i, t + 1, RIM + rows : 2 * RIM + rows, :] = below[rim, at]
             return 0
 
-        lax.fori_loop(c * per, (c + 1) * per, fill_rim, 0)
+        lax.fori_loop(starts[c], starts[c + 1], fill_rim, 0)
         render_rim(c)
 
     for level in range(1, levels):

time: 22.2 us -> 22.1 us (level)
  no operation moved by 1% of the time
where the time goes in v4:
time: 22.1 us; the launch traced here: 21.9 us
  Pallas kernels  21.9 us (99%)
    pallas_call x1, Pallas kernels, on_device(): pl.pallas_call(functools.partial(kernel, (n_depth, n_tile, halo_chunks)),...  21.1 us
    pallas_call x1, Pallas kernels, on_device(): pl.pallas_call(store, out_shape=jax.ShapeDtypeStruct((4, rows, cols), jnp...  0.8 us

profile of v4, /device:TPU:13, one launch (start us, length us, event | category | flops | bytes accessed | tf_op | source)
XLA Modules:
  0.0 21.9 jit_solution(2244746504098854895)
XLA Ops:
  0.0 21.1 %shard_map.73.held = f32[4,32,1024]{2,1,0:T(8,128)S(1)} custom-call(bf16[16,32,1024]{2,1,0:T(8,128)(2,1)} %stored.1, s32[16]{0:T(128)} %row_shift_arg.1, s32[4]{0:T(128)} %brick_order_arg.1, f32[4]{0:T(128)} %gain_arg.1, f32[4]{0:T(128)} %bias_arg.1, f32[3]{0:T(128)} %light_arg.1, f32[3]{0:T(128)} %background_arg.1), custom_call_target="tpu_custom_call" | custom-call | tf_op jit(solution)/shard_map/pallas_call | solution.py:387
  21.1 0.8 %shard_map.74 = f32[4,32,1024]{2,1,0:T(8,128)} custom-call(f32[4,32,1024]{2,1,0:T(8,128)S(1)} %shard_map.73.held), custom_call_target="tpu_custom_call" | custom-call | tf_op jit(solution)/shard_map/pallas_call | solution.py:412
